TPU v7x, 32 devices: a whole 2x2x4 slice. The times are simulated.
32 devices in a mesh: patch: 8 (over z, x), sub: 4 (over y, core).
Axes of the slice: x: 2, y: 2, z: 4, core: 2. Of those that a mesh axis runs over, the one named last changes fastest.
Arguments:
- displacement: float32 [3, 64, 8192], P(None, 'patch', 'sub'), may hold values from -3 to 3
- load: float32 [3, 64, 8192], P(None, 'patch', 'sub'), may hold values from -6 to 6
- foundation: float32 [3, 64, 8192], P(None, 'patch', 'sub'), may hold values from 0.2 to 2
- layup: int32 [64, 8192], P('patch', 'sub'), may hold values from 0 to 7
- layup_stiffness: float32 [8, 6, 6], replicated, as said below
- w_first: bfloat16 [128, 6], replicated, may hold values from -2.5 to 2.5
- w_mid: bfloat16 [3, 128, 128], replicated, may hold values from -0.5 to 0.5
- w_last: bfloat16 [6, 128], replicated, may hold values from -0.5 to 0.5
Outputs:
- residual: float32 [3, 64, 8192], P(None, 'patch', 'sub')
- adjoint: float32 [3, 64, 8192], P(None, 'patch', 'sub')
- grad_first: float32 [128, 6], replicated
- grad_mid: float32 [3, 128, 128], replicated
- grad_last: float32 [6, 128], replicated
Inputs may be any that keep to these rules, and one draw needn't show every extreme that they name: `layup_stiffness`: each of the 8 matrices is symmetric positive definite.
All inputs are finite; a program needn't handle non-finite values.
Results may differ from a plain program's by a relative error of at most 0.0006.
The roundings to bfloat16 on the way count: a program that leaves them out, or rounds other values in their place, can miss the bound.
Values sent between devices are 32-bit elements; how exact they have to be, the bound alone decides.
No kernel may reach another device: no remote copies, remote signals or barrier semaphores. Data moves between devices by JAX's collectives and lax.ppermute only.
A program may use at most 128 MiB of HBM per device.

v0:
```python
import jax
import jax.numpy as jnp
from jax import lax
from jax.sharding import PartitionSpec as P

ITERS = 4
BASIS_VALUE = (0.125, 0.75, 0.125)
BASIS_SLOPE = (-0.5, 0.0, 0.5)
BASIS_CURVE = (1.0, -2.0, 1.0)
HOOP_CURVATURE = 0.25


def padded_2(cells, sides, width):
    for axis, dim in sides:
        count = lax.axis_size(axis)
        head = lax.slice_in_dim(cells, 0, width, axis=dim)
        tail = lax.slice_in_dim(cells, cells.shape[dim] - width, cells.shape[dim], axis=dim)
        cells = jnp.concatenate(
            [
                lax.ppermute(tail, axis, [(i, (i + 1) % count) for i in range(count)]),
                cells,
                lax.ppermute(head, axis, [((i + 1) % count, i) for i in range(count)]),
            ],
            axis=dim,
        )
    return cells


def correlate(padded, along_x, along_y):
    row_count = padded.shape[-2] - 2
    col_count = padded.shape[-1] - 2
    partial_x = None
    for offset in range(3):
        if along_x[offset] != 0.0:
            weighted = along_x[offset] * padded[..., offset : offset + row_count, :]
            partial_x = weighted if partial_x is None else partial_x + weighted
    running = None
    for offset in range(3):
        if along_y[offset] != 0.0:
            weighted = along_y[offset] * partial_x[..., offset : offset + col_count]
            running = weighted if running is None else running + weighted
    return running


def mirrored(padded, along_x, along_y):
    return correlate(padded, along_x[::-1], along_y[::-1])


def strains(padded):
    along_u, along_v, along_w = (padded[0], padded[1], padded[2])
    return jnp.stack(
        [
            correlate(along_u, BASIS_SLOPE, BASIS_VALUE),
            correlate(along_v, BASIS_VALUE, BASIS_SLOPE)
            + HOOP_CURVATURE * correlate(along_w, BASIS_VALUE, BASIS_VALUE),
            correlate(along_u, BASIS_VALUE, BASIS_SLOPE)
            + correlate(along_v, BASIS_SLOPE, BASIS_VALUE),
            -correlate(along_w, BASIS_CURVE, BASIS_VALUE),
            -correlate(along_w, BASIS_VALUE, BASIS_CURVE),
            -2.0 * correlate(along_w, BASIS_SLOPE, BASIS_SLOPE),
        ]
    )


def forces(spread):
    force_u = mirrored(spread[0], BASIS_SLOPE, BASIS_VALUE) + mirrored(
        spread[2], BASIS_VALUE, BASIS_SLOPE
    )
    force_v = mirrored(spread[1], BASIS_VALUE, BASIS_SLOPE) + mirrored(
        spread[2], BASIS_SLOPE, BASIS_VALUE
    )
    force_w = (
        HOOP_CURVATURE * mirrored(spread[1], BASIS_VALUE, BASIS_VALUE)
        - mirrored(spread[3], BASIS_CURVE, BASIS_VALUE)
        - mirrored(spread[4], BASIS_VALUE, BASIS_CURVE)
        - 2.0 * mirrored(spread[5], BASIS_SLOPE, BASIS_SLOPE)
    )
    return jnp.stack([force_u, force_v, force_w])


def apply_layup(stiffness_map, strain):
    running = stiffness_map[:, 0] * strain[0]
    for column in range(1, 6):
        running = running + stiffness_map[:, column] * strain[column]
    return running


def outer_product(left, right):
    return lax.dot_general(
        left, right, (((1,), (1,)), ((), ())), preferred_element_type=jnp.float32
    )


def forward_mlp(inputs, w_first, w_mid, w_last):
    hidden_layer = jnp.tanh(jnp.dot(w_first, inputs, preferred_element_type=jnp.float32)).astype(
        jnp.bfloat16
    )
    activations = [hidden_layer]
    for layer_index in range(w_mid.shape[0]):
        hidden_layer = jnp.tanh(
            jnp.dot(w_mid[layer_index], hidden_layer, preferred_element_type=jnp.float32)
        ).astype(jnp.bfloat16)
        activations.append(hidden_layer)
    return (jnp.dot(w_last, hidden_layer, preferred_element_type=jnp.float32), activations)


def backward_mlp(inputs, activations, upstream, w_mid, w_last):
    grad_last = outer_product(upstream, activations[-1])
    signal = jnp.dot(w_last.T, upstream, preferred_element_type=jnp.float32)
    derivative = (signal * (1.0 - jnp.square(activations[-1].astype(jnp.float32)))).astype(
        jnp.bfloat16
    )
    mid_grads = []
    for layer_index in range(w_mid.shape[0] - 1, -1, -1):
        mid_grads.append(outer_product(derivative, activations[layer_index]))
        signal = jnp.dot(w_mid[layer_index].T, derivative, preferred_element_type=jnp.float32)
        derivative = (
            signal * (1.0 - jnp.square(activations[layer_index].astype(jnp.float32)))
        ).astype(jnp.bfloat16)
    grad_first = outer_product(derivative, inputs)
    return (grad_first, jnp.stack(mid_grads[::-1]), grad_last)


def two_products(remainder, mapped):
    return lax.psum((jnp.sum(remainder * remainder), jnp.sum(remainder * mapped)), ("patch", "sub"))


def per_device(displacement, load, foundation, layup, layup_stiffness, w_first, w_mid, w_last):
    layup_count = layup_stiffness.shape[0]
    onehot = (layup[None] == jnp.arange(layup_count, dtype=jnp.int32)[:, None, None]).astype(
        jnp.float32
    )
    stiffness_map = jnp.einsum(
        "lab,lxy->abxy", layup_stiffness, onehot, precision=lax.Precision.HIGHEST
    )

    def operate(search):
        padded = padded_2(search, (("patch", 1), ("sub", 2)), 1)
        element_stress = apply_layup(stiffness_map, strains(padded))
        spread = padded_2(element_stress, (("patch", 1), ("sub", 2)), 1)
        return forces(spread) + foundation * search

    padded = padded_2(displacement, (("patch", 1), ("sub", 2)), 1)
    strain = strains(padded)
    inputs = strain.reshape(6, -1).astype(jnp.bfloat16)
    learned, activations = forward_mlp(inputs, w_first, w_mid, w_last)
    stress = apply_layup(stiffness_map, strain) + learned.reshape(strain.shape)
    spread = padded_2(stress, (("patch", 1), ("sub", 2)), 1)
    residual = forces(spread) + foundation * displacement - load
    adjoint = jnp.zeros_like(residual)
    remainder = residual
    mapped = operate(remainder)
    norm_now, curved = two_products(remainder, mapped)
    step_size = norm_now / curved
    direction, mapped_dir = (remainder, mapped)
    for step_index in range(ITERS):
        adjoint = adjoint + step_size * direction
        remainder = remainder - step_size * mapped_dir
        if step_index + 1 < ITERS:
            mapped = operate(remainder)
            norm_next, curved = two_products(remainder, mapped)
            beta_ratio = norm_next / norm_now
            step_size = norm_next / (curved - beta_ratio * norm_next / step_size)
            direction = remainder + beta_ratio * direction
            mapped_dir = mapped + beta_ratio * mapped_dir
            norm_now = norm_next
    cycle = padded_2(adjoint, (("patch", 1), ("sub", 2)), 1)
    upstream = strains(cycle).reshape(6, -1).astype(jnp.bfloat16)
    grad_first, grad_mid, grad_last = backward_mlp(inputs, activations, upstream, w_mid, w_last)
    totals = lax.psum((grad_first, grad_mid, grad_last), ("patch", "sub"))
    return (residual, adjoint, totals[0], totals[1], totals[2])


def solution(mesh):
    in_specs = (
        P(None, "patch", "sub"),
        P(None, "patch", "sub"),
        P(None, "patch", "sub"),
        P("patch", "sub"),
        P(),
        P(),
        P(),
        P(),
    )
    out_specs = (P(None, "patch", "sub"), P(None, "patch", "sub"), P(), P(), P())
    return jax.shard_map(
        per_device, mesh=mesh, in_specs=in_specs, out_specs=out_specs, check_vma=False
    )
```

profile of v0, /device:TPU:8, one launch (start us, length us, event | category | flops | bytes accessed | tf_op | source)
XLA Modules:
  0.0 525.6 jit_solution(10310662434873777303)
XLA Ops:
  11.3 2.6 convolution_bitcast_fusion
  15.5 2.2 fusion.366
  20.4 2.5 fusion.3
  22.9 2.0 copy-done.5
  33.1 2.2 collective-permute-start.4
  41.8 2.1 collective-permute-done.6
  47.2 1.8 collective-permute-start.8
  50.2 1.8 collective-permute-done.8
  59.6 2.3 collective-permute-start.12
  62.6 2.1 collective-permute-done.12
  68.8 1.8 collective-permute-done.14
  70.7 2.3 concatenate.77
  75.7 44.3 %all-reduce.4 = (f32[]{:T(128)}, f32[]{:T(128)}) all-reduce(f32[]{:T(128)} %get-tuple-element.12, f32[]{:T(128)} %get-tuple-element.11), channel_id=1, replica_groups=mesh['patch'=8,'sub'=4] {'patch','sub'}, use_global_device_ids=true, to_apply=%region_1.0 | all-reduce | flops 2 | bytes 16 | tf_op jit(solution)/shard_map/psum | solution.py:125
  121.4 2.3 collective-permute-start.16
  124.4 1.8 collective-permute-done.16
  129.3 2.0 collective-permute-done.18
  134.6 2.3 collective-permute-start.20
  137.5 2.1 collective-permute-done.20
  143.8 2.2 collective-permute-done.22
  146.0 2.3 concatenate.81
  151.1 41.7 %all-reduce.3 = (f32[]{:T(128)}, f32[]{:T(128)}) all-reduce(f32[]{:T(128)} %get-tuple-element.10, f32[]{:T(128)} %get-tuple-element.9), channel_id=1, replica_groups=mesh['patch'=8,'sub'=4] {'patch','sub'}, use_global_device_ids=true, to_apply=%region_5.0 | all-reduce | flops 2 | bytes 16 | tf_op jit(solution)/shard_map/psum | solution.py:125
  198.3 2.3 collective-permute-start.24
  201.3 1.8 collective-permute-done.24
  206.9 2.0 collective-permute-done.26
  208.9 1.9 concatenate.83
  214.1 2.6 collective-permute-start.28
  217.1 2.1 collective-permute-done.28
  223.7 2.3 collective-permute-done.30
  226.0 2.3 concatenate.85
  231.6 41.5 %all-reduce.2 = (f32[]{:T(128)}, f32[]{:T(128)}) all-reduce(f32[]{:T(128)} %get-tuple-element.8, f32[]{:T(128)} %get-tuple-element.7), channel_id=1, replica_groups=mesh['patch'=8,'sub'=4] {'patch','sub'}, use_global_device_ids=true, to_apply=%region_9.0 | all-reduce | flops 2 | bytes 16 | tf_op jit(solution)/shard_map/psum | solution.py:125
  278.4 2.3 collective-permute-start.32
  281.3 1.8 collective-permute-done.32
  286.9 1.9 collective-permute-done.34
  288.8 1.9 concatenate.87
  294.1 2.3 collective-permute-start.36
  297.1 2.1 collective-permute-done.36
  302.4 2.3 collective-permute-done.38
  306.3 41.7 %all-reduce.1 = (f32[]{:T(128)}, f32[]{:T(128)}) all-reduce(f32[]{:T(128)} %get-tuple-element.6, f32[]{:T(128)} %get-tuple-element.5), channel_id=1, replica_groups=mesh['patch'=8,'sub'=4] {'patch','sub'}, use_global_device_ids=true, to_apply=%region_13.0 | all-reduce | flops 2 | bytes 16 | tf_op jit(solution)/shard_map/psum | solution.py:125
  352.1 2.3 collective-permute-start.40
  355.1 1.8 collective-permute-done.40
  359.9 1.9 collective-permute-done.42
  363.9 4.4 fusion.7
  373.2 3.7 fusion.1
  376.9 5.6 %fusion.8 = f32[128,6]{0,1:T(8,128)S(1)} fusion(bf16[6,16384]{1,0:T(8,128)(2,1)S(1)} %copy-done.20, bf16[16384,128]{1,0:T(8,128)(2,1)} %fusion.1, bf16[16384,128]{1,0:T(8,128)(2,1)} %copy-done.5, bf16[3,128,128]{2,1,0:T(8,128)(2,1)S(1)} %copy-done.29), kind=kOutput, calls=%fused_computation.17 | convolution fusion | flops 572522496 | bytes 8686592 | tf_op jit(solution)/shard_map/dot_general | solution.py:89
  382.5 4.8 convolution_bitcast_fusion.3
  388.0 2.8 fusion.390
  390.8 41.5 %all-reduce = (f32[128,6]{0,1:T(8,128)}, f32[6,128]{1,0:T(8,128)}) all-reduce(f32[128,6]{0,1:T(8,128)S(1)} %fusion.8, f32[6,128]{1,0:T(8,128)S(1)} %fusion.390), channel_id=1, replica_groups=mesh['patch'=8,'sub'=4] {'patch','sub'}, use_global_device_ids=true, to_apply=%region_16.0 | all-reduce | flops 1536 | bytes 12288 | tf_op jit(solution)/shard_map/psum | solution.py:170
  432.4 84.5 %all-reduce.7.cloned.1.call-done = f32[3,128,128]{2,1,0:T(8,128)} async-done(((f32[3,128,128]{2,1,0:T(8,128)}), f32[3,128,128]{2,1,0:T(8,128)}) %all-reduce.7.cloned.1.call-update) | async-done | bytes 196624 | tf_op jit(solution)/shard_map/psum | solution.py:170
  (248 shorter events, 101.2 us)
Async XLA Ops:
  7.2 509.7 %all-reduce.7.cloned.1.call-start = ((), (), s32[]{:S(2)}) async-start(), calls=%async_computation | async-start | bytes 393216 | tf_op jit(solution)/shard_map/psum | solution.py:170
  8.3 5.6 %collective-permute-start = (f32[3,1,2048]{2,1,0:T(1,128)S(1)}, f32[3,1,2048]{2,1,0:T(1,128)S(1)}, u32[]{:S(2)}, u32[]{:S(2)}) collective-permute-start(f32[3,1,2048]{2,1,0:T(1,128)S(1)} %get-tuple-element.160), channel_id=1, source_target_pairs={{0,4},{4,8},{8,12},{12,16},{16,20},{20,24},{24,28},{28,0},{1,5},{5... | collective-permute-start | bytes 73736 | tf_op jit(solution)/shard_map/ppermute | solution.py:20
  9.8 4.1 collective-permute-start.1
  15.0 2.7 collective-permute-start.3
  15.4 3.3 collective-permute-start.2
  33.1 5.0 collective-permute-start.4
  35.3 4.5 collective-permute-start.5
  40.1 1.8 collective-permute-start.7
  40.1 3.9 collective-permute-start.6
  47.1 304.8 %copy-start.8 = (f32[3,8,2048]{2,1,0:T(8,128)}, f32[3,8,2048]{2,1,0:T(8,128)S(1)}, u32[]{:S(2)}) copy-start(f32[3,8,2048]{2,1,0:T(8,128)S(1)} %fusion.37) | copy-start | bytes 589828
  47.2 4.8 collective-permute-start.8
  49.0 3.8 collective-permute-start.9
  53.0 1.5 collective-permute-start.11
  53.0 3.3 collective-permute-start.10
  59.6 5.0 collective-permute-start.12
  61.9 4.1 collective-permute-start.13
  67.1 1.8 collective-permute-start.15
  67.1 3.6 collective-permute-start.14
  121.4 4.8 collective-permute-start.16
  123.7 3.8 collective-permute-start.17
  127.7 1.5 collective-permute-start.19
  127.7 3.5 collective-permute-start.18
  134.6 5.1 collective-permute-start.20
  136.8 4.1 collective-permute-start.21
  142.0 1.8 collective-permute-start.23
  142.0 4.0 collective-permute-start.22
  150.3 63.7 %copy-start.21 = (f32[1,8,2048]{2,1,0:T(8,128)}, f32[1,8,2048]{2,1,0:T(8,128)S(1)}, u32[]{:S(2)}) copy-start(f32[1,8,2048]{2,1,0:T(8,128)S(1)} %get-tuple-element.172) | copy-start | bytes 196612
  150.4 63.7 %copy-start.22 = (f32[1,8,2048]{2,1,0:T(8,128)}, f32[1,8,2048]{2,1,0:T(8,128)S(1)}, u32[]{:S(2)}) copy-start(f32[1,8,2048]{2,1,0:T(8,128)S(1)} %get-tuple-element.173) | copy-start | bytes 196612
  198.3 4.8 collective-permute-start.24
  200.7 3.8 collective-permute-start.25
  205.4 1.5 collective-permute-start.27
  205.4 3.5 collective-permute-start.26
  214.1 5.0 collective-permute-start.28
  216.7 4.1 collective-permute-start.29
  221.9 1.8 collective-permute-start.31
  221.9 4.1 collective-permute-start.30
  278.4 4.8 collective-permute-start.32
  280.7 3.8 collective-permute-start.33
  285.4 1.5 collective-permute-start.35
  285.4 3.4 collective-permute-start.34
  294.1 5.1 collective-permute-start.36
  296.3 4.1 collective-permute-start.37
  300.7 1.8 collective-permute-start.39
  300.7 4.0 collective-permute-start.38
  352.1 4.8 collective-permute-start.40
  354.4 3.8 collective-permute-start.41
  358.4 1.5 collective-permute-start.43
  358.4 3.4 collective-permute-start.42
  (28 other events, 245.9 us)
Sparse Core Ops, SparseCore 0:
  388.1 128.7 all-reduce.6
where the time goes:
time: 535 us; the launch traced here: 526 us
  blocking collectives  211 us (39%)
  waiting for transfers between devices  149 us (28%)
  starting transfers between devices  39 us (7%)
  matrix products  35.5 us (7%)
  local copies, waits for them, and re-layouts  33.1 us (6%)
  between operations  29.3 us (5%)
  other arithmetic  28.6 us (5%)
    psum x4, blocking collectives, two_products(): lax.psum((jnp.sum(remainder * remainder), jnp.sum(remainder * mapped)), (...  169 us
    psum x1, waiting for transfers between devices, per_device(): totals = lax.psum((grad_first, grad_mid, grad_last), ('patch', 'sub'))  84.5 us
    psum x1, blocking collectives, per_device(): totals = lax.psum((grad_first, grad_mid, grad_last), ('patch', 'sub'))  41.5 us
    ppermute x22, waiting for transfers between devices, padded_2(): lax.ppermute(tail, axis, [(i, (i + 1) % count) for i in range(count)])  40.1 us
    ppermute x22, starting transfers between devices, padded_2(): lax.ppermute(tail, axis, [(i, (i + 1) % count) for i in range(count)])  29.5 us
    ppermute x22, waiting for transfers between devices, padded_2(): lax.ppermute(head, axis, [((i + 1) % count, i) for i in range(count)])  24.7 us
    concatenate x11, local copies, waits for them, and re-layouts, padded_2(): jnp.concatenate([lax.ppermute(tail, axis, [(i, (i + 1) % count) for i in...  15.9 us
    dot_general x5, matrix products, outer_product(): lax.dot_general(left, right, (((1,), (1,)), ((), ())), preferred_element_...  15.9 us
  transfers between devices with their start and end apart: 45, of which 42 were waited for; matrix products, arithmetic and copies ran while one was open for 1% of the time, Pallas kernels for 0%

commit v1 on v0

--- a/solution.py
+++ b/solution.py
@@ -167,7 +167,9 @@
     cycle = padded_2(adjoint, (("patch", 1), ("sub", 2)), 1)
     upstream = strains(cycle).reshape(6, -1).astype(jnp.bfloat16)
     grad_first, grad_mid, grad_last = backward_mlp(inputs, activations, upstream, w_mid, w_last)
-    totals = lax.psum((grad_first, grad_mid, grad_last), ("patch", "sub"))
+    totals = (grad_first, grad_mid, grad_last)
+    for mesh_axis in ("patch", "sub"):
+        totals = lax.psum(totals, mesh_axis)
     return (residual, adjoint, totals[0], totals[1], totals[2])
 
 

time: 535 us -> 505 us (0.944)
  the two profiles are of different devices: /device:TPU:8 before, /device:TPU:0 now
where the time goes in v1:
time: 505 us; the launch traced here: 495 us
  blocking collectives  186 us (37%)
  waiting for transfers between devices  125 us (25%)
  starting transfers between devices  61.2 us (12%)
  local copies, waits for them, and re-layouts  34.3 us (7%)
  matrix products  29.9 us (6%)
  between operations  29.7 us (6%)
  other arithmetic  28.6 us (6%)
    psum x4, blocking collectives, two_products(): lax.psum((jnp.sum(remainder * remainder), jnp.sum(remainder * mapped)), (...  159 us
    psum x2, waiting for transfers between devices, per_device(): totals = lax.psum(totals, mesh_axis)  70.5 us
    ppermute x22, waiting for transfers between devices, padded_2(): lax.ppermute(tail, axis, [(i, (i + 1) % count) for i in range(count)])  43.7 us
    ppermute x22, starting transfers between devices, padded_2(): lax.ppermute(head, axis, [((i + 1) % count, i) for i in range(count)])  37.1 us
    psum x2, blocking collectives, per_device(): totals = lax.psum(totals, mesh_axis)  26.3 us
    ppermute x22, starting transfers between devices, padded_2(): lax.ppermute(tail, axis, [(i, (i + 1) % count) for i in range(count)])  23.7 us
    concatenate x11, local copies, waits for them, and re-layouts, padded_2(): jnp.concatenate([lax.ppermute(tail, axis, [(i, (i + 1) % count) for i in...  15.9 us
    unnamed x79, local copies, waits for them, and re-layouts  12.6 us
  transfers between devices with their start and end apart: 46, of which 36 were waited for; matrix products, arithmetic and copies ran while one was open for 3% of the time, Pallas kernels for 0%

profile of v1, /device:TPU:0, one launch (start us, length us, event | category | flops | bytes accessed | tf_op | source)
XLA Modules:
  0.0 494.8 jit_solution(3368392117163665084)
XLA Ops:
  8.3 3.0 collective-permute-start
  11.3 3.1 collective-permute-start.1
  14.4 2.6 convolution_bitcast_fusion
  18.8 2.2 fusion.366
  23.9 2.5 fusion.3
  26.4 2.0 copy-done.5
  36.8 4.7 collective-permute-start.5
  50.6 5.0 %collective-permute-start.9 = (f32[3,1,2048]{2,1,0:T(1,128)S(1)}, f32[3,1,2048]{2,1,0:T(1,128)S(1)}, u32[]{:S(2)}, u32[]{:S(2)}) collective-permute-start(f32[3,1,2048]{2,1,0:T(1,128)S(1)} %get-tuple-element.161), channel_id=1, source_target_pairs={{4,0},{8,4},{12,8},{16,12},{20,16},{24,20},{28,24},{0,28},{5,1},{9... | collective-permute-start | bytes 73736 | tf_op jit(solution)/shard_map/ppermute | solution.py:22
  64.1 4.8 collective-permute-start.13
  69.0 2.0 collective-permute-done.12
  75.7 2.3 concatenate.77
  80.7 39.9 %all-reduce.3 = (f32[]{:T(128)}, f32[]{:T(128)}) all-reduce(f32[]{:T(128)} %get-tuple-element.12, f32[]{:T(128)} %get-tuple-element.11), channel_id=1, replica_groups=mesh['patch'=8,'sub'=4] {'patch','sub'}, use_global_device_ids=true, to_apply=%region_1.0 | all-reduce | flops 2 | bytes 16 | tf_op jit(solution)/shard_map/psum | solution.py:125
  122.0 2.3 collective-permute-start.16
  124.3 2.4 collective-permute-start.17
  130.2 2.7 collective-permute-done.18
  136.3 1.9 collective-permute-start.20
  138.2 2.9 collective-permute-start.21
  141.1 2.1 collective-permute-done.20
  146.2 2.2 collective-permute-done.22
  148.5 2.3 concatenate.81
  153.5 39.8 %all-reduce.2 = (f32[]{:T(128)}, f32[]{:T(128)}) all-reduce(f32[]{:T(128)} %get-tuple-element.10, f32[]{:T(128)} %get-tuple-element.9), channel_id=1, replica_groups=mesh['patch'=8,'sub'=4] {'patch','sub'}, use_global_device_ids=true, to_apply=%region_5.0 | all-reduce | flops 2 | bytes 16 | tf_op jit(solution)/shard_map/psum | solution.py:125
  198.9 2.3 collective-permute-start.24
  201.3 2.4 collective-permute-start.25
  207.9 3.1 collective-permute-done.26
  211.0 1.9 concatenate.83
  218.1 3.0 collective-permute-start.29
  221.1 2.0 collective-permute-done.28
  226.1 2.2 collective-permute-done.30
  228.3 2.3 concatenate.85
  233.9 39.8 %all-reduce.1 = (f32[]{:T(128)}, f32[]{:T(128)}) all-reduce(f32[]{:T(128)} %get-tuple-element.8, f32[]{:T(128)} %get-tuple-element.7), channel_id=1, replica_groups=mesh['patch'=8,'sub'=4] {'patch','sub'}, use_global_device_ids=true, to_apply=%region_9.0 | all-reduce | flops 2 | bytes 16 | tf_op jit(solution)/shard_map/psum | solution.py:125
  279.0 2.3 collective-permute-start.32
  281.3 2.4 collective-permute-start.33
  288.0 2.6 collective-permute-done.34
  290.6 1.9 concatenate.87
  297.7 3.0 collective-permute-start.37
  300.7 2.1 collective-permute-done.36
  304.8 2.3 collective-permute-done.38
  308.7 39.8 %all-reduce = (f32[]{:T(128)}, f32[]{:T(128)}) all-reduce(f32[]{:T(128)} %get-tuple-element.6, f32[]{:T(128)} %get-tuple-element.5), channel_id=1, replica_groups=mesh['patch'=8,'sub'=4] {'patch','sub'}, use_global_device_ids=true, to_apply=%region_13.0 | all-reduce | flops 2 | bytes 16 | tf_op jit(solution)/shard_map/psum | solution.py:125
  352.7 2.3 collective-permute-start.40
  355.0 2.4 collective-permute-start.41
  361.0 3.0 collective-permute-done.42
  365.9 4.4 fusion.7
  380.5 5.6 %fusion.8 = f32[128,6]{0,1:T(8,128)S(1)} fusion(bf16[6,16384]{1,0:T(8,128)(2,1)S(1)} %copy-done.22, bf16[16384,128]{1,0:T(8,128)(2,1)} %copy-done.8, bf16[16384,128]{1,0:T(8,128)(2,1)} %copy-done.5, bf16[3,128,128]{2,1,0:T(8,128)(2,1)S(1)} %copy-done.31), kind=kOutput, calls=%fused_computation.17 | convolution fusion | flops 572522496 | bytes 8686592 | tf_op jit(solution)/shard_map/dot_general | solution.py:89
  386.1 66.2 %all-reduce.9.cloned.1.call-done = f32[3,128,128]{2,1,0:T(8,128)} async-done(((f32[3,128,128]{2,1,0:T(8,128)}), f32[3,128,128]{2,1,0:T(8,128)}) %all-reduce.9.cloned.1.call-update) | async-done | bytes 196624 | tf_op jit(solution)/shard_map/psum | solution.py:172
  452.4 2.8 fusion.390
  455.2 19.8 %all-reduce.4 = (f32[128,6]{0,1:T(8,128)S(1)}, f32[6,128]{1,0:T(8,128)S(1)}) all-reduce(f32[128,6]{0,1:T(8,128)S(1)} %fusion.8, f32[6,128]{1,0:T(8,128)S(1)} %fusion.390), channel_id=1, replica_groups=mesh['patch'=8,'sub'=4] {'patch'}, use_global_device_ids=true, to_apply=%region_16.0 | all-reduce | flops 1536 | bytes 12288 | tf_op jit(solution)/shard_map/psum | solution.py:172
  475.0 6.5 %all-reduce.5 = (f32[128,6]{0,1:T(8,128)}, f32[6,128]{1,0:T(8,128)}) all-reduce(f32[128,6]{0,1:T(8,128)S(1)} %get-tuple-element.21, f32[6,128]{1,0:T(8,128)S(1)} %get-tuple-element.22), channel_id=1, replica_groups=mesh['patch'=8,'sub'=4] {'sub'}, use_global_device_ids=true, to_apply=%region_17.0 | all-reduce | flops 1536 | bytes 12288 | tf_op jit(solution)/shard_map/psum | solution.py:172
  481.5 4.3 all-reduce.11.cloned.1.call-done
  (256 shorter events, 99.0 us)
Async XLA Ops:
  7.2 445.2 %all-reduce.9.cloned.1.call-start = ((), (), s32[]{:S(2)}) async-start(), calls=%async_computation | async-start | bytes 393216 | tf_op jit(solution)/shard_map/psum | solution.py:172
  8.3 8.7 %collective-permute-start = (f32[3,1,2048]{2,1,0:T(1,128)S(1)}, f32[3,1,2048]{2,1,0:T(1,128)S(1)}, u32[]{:S(2)}, u32[]{:S(2)}) collective-permute-start(f32[3,1,2048]{2,1,0:T(1,128)S(1)} %get-tuple-element.162), channel_id=1, source_target_pairs={{0,4},{4,8},{8,12},{12,16},{16,20},{20,24},{24,28},{28,0},{1,5},{5... | collective-permute-start | bytes 73736 | tf_op jit(solution)/shard_map/ppermute | solution.py:20
  11.3 5.7 %collective-permute-start.1 = (f32[3,1,2048]{2,1,0:T(1,128)S(1)}, f32[3,1,2048]{2,1,0:T(1,128)S(1)}, u32[]{:S(2)}, u32[]{:S(2)}) collective-permute-start(f32[3,1,2048]{2,1,0:T(1,128)S(1)} %get-tuple-element.163), channel_id=1, source_target_pairs={{4,0},{8,4},{12,8},{16,12},{20,16},{24,20},{28,24},{0,28},{5,1},{9... | collective-permute-start | bytes 73736 | tf_op jit(solution)/shard_map/ppermute | solution.py:22
  18.1 2.9 collective-permute-start.3
  18.8 3.3 collective-permute-start.2
  36.6 6.8 %collective-permute-start.4 = (f32[6,1,2048]{2,1,0:T(1,128)S(1)}, f32[6,1,2048]{2,1,0:T(1,128)S(1)}, u32[]{:S(2)}, u32[]{:S(2)}) collective-permute-start(f32[6,1,2048]{2,1,0:T(1,128)S(1)} %get-tuple-element.148), channel_id=1, source_target_pairs={{0,4},{4,8},{8,12},{12,16},{16,20},{20,24},{24,28},{28,0},{1,5},{5... | collective-permute-start | bytes 147464 | tf_op jit(solution)/shard_map/ppermute | solution.py:20
  36.8 6.6 %collective-permute-start.5 = (f32[6,1,2048]{2,1,0:T(1,128)S(1)}, f32[6,1,2048]{2,1,0:T(1,128)S(1)}, u32[]{:S(2)}, u32[]{:S(2)}) collective-permute-start(f32[6,1,2048]{2,1,0:T(1,128)S(1)} %get-tuple-element.149), channel_id=1, source_target_pairs={{4,0},{8,4},{12,8},{16,12},{20,16},{24,20},{28,24},{0,28},{5,1},{9... | collective-permute-start | bytes 147464 | tf_op jit(solution)/shard_map/ppermute | solution.py:22
  43.6 1.8 collective-permute-start.7
  43.7 3.6 collective-permute-start.6
  50.5 302.1 %copy-start.10 = (f32[3,8,2048]{2,1,0:T(8,128)}, f32[3,8,2048]{2,1,0:T(8,128)S(1)}, u32[]{:S(2)}) copy-start(f32[3,8,2048]{2,1,0:T(8,128)S(1)} %fusion.37) | copy-start | bytes 589828
  50.5 6.8 %collective-permute-start.8 = (f32[3,1,2048]{2,1,0:T(1,128)S(1)}, f32[3,1,2048]{2,1,0:T(1,128)S(1)}, u32[]{:S(2)}, u32[]{:S(2)}) collective-permute-start(f32[3,1,2048]{2,1,0:T(1,128)S(1)} %get-tuple-element.160), channel_id=1, source_target_pairs={{0,4},{4,8},{8,12},{12,16},{16,20},{20,24},{24,28},{28,0},{1,5},{5... | collective-permute-start | bytes 73736 | tf_op jit(solution)/shard_map/ppermute | solution.py:20
  50.6 6.7 %collective-permute-start.9 = (f32[3,1,2048]{2,1,0:T(1,128)S(1)}, f32[3,1,2048]{2,1,0:T(1,128)S(1)}, u32[]{:S(2)}, u32[]{:S(2)}) collective-permute-start(f32[3,1,2048]{2,1,0:T(1,128)S(1)} %get-tuple-element.161), channel_id=1, source_target_pairs={{4,0},{8,4},{12,8},{16,12},{20,16},{24,20},{28,24},{0,28},{5,1},{9... | collective-permute-start | bytes 73736 | tf_op jit(solution)/shard_map/ppermute | solution.py:22
  57.4 1.5 collective-permute-start.11
  57.5 3.3 collective-permute-start.10
  64.1 6.9 %collective-permute-start.12 = (f32[6,1,2048]{2,1,0:T(1,128)S(1)}, f32[6,1,2048]{2,1,0:T(1,128)S(1)}, u32[]{:S(2)}, u32[]{:S(2)}) collective-permute-start(f32[6,1,2048]{2,1,0:T(1,128)S(1)} %get-tuple-element.144), channel_id=1, source_target_pairs={{0,4},{4,8},{8,12},{12,16},{16,20},{20,24},{24,28},{28,0},{1,5},{5... | collective-permute-start | bytes 147464 | tf_op jit(solution)/shard_map/ppermute | solution.py:20
  64.1 6.8 %collective-permute-start.13 = (f32[6,1,2048]{2,1,0:T(1,128)S(1)}, f32[6,1,2048]{2,1,0:T(1,128)S(1)}, u32[]{:S(2)}, u32[]{:S(2)}) collective-permute-start(f32[6,1,2048]{2,1,0:T(1,128)S(1)} %get-tuple-element.145), channel_id=1, source_target_pairs={{4,0},{8,4},{12,8},{16,12},{20,16},{24,20},{28,24},{0,28},{5,1},{9... | collective-permute-start | bytes 147464 | tf_op jit(solution)/shard_map/ppermute | solution.py:22
  72.1 1.8 collective-permute-start.15
  72.1 3.6 collective-permute-start.14
  122.0 6.6 %collective-permute-start.16 = (f32[3,1,2048]{2,1,0:T(1,128)S(1)}, f32[3,1,2048]{2,1,0:T(1,128)S(1)}, u32[]{:S(2)}, u32[]{:S(2)}) collective-permute-start(f32[3,1,2048]{2,1,0:T(1,128)S(1)} %get-tuple-element.158), channel_id=1, source_target_pairs={{0,4},{4,8},{8,12},{12,16},{16,20},{20,24},{24,28},{28,0},{1,5},{5... | collective-permute-start | bytes 73736 | tf_op jit(solution)/shard_map/ppermute | solution.py:20
  124.3 4.3 collective-permute-start.17
  128.7 1.5 collective-permute-start.19
  128.7 4.3 collective-permute-start.18
  136.3 6.9 %collective-permute-start.20 = (f32[6,1,2048]{2,1,0:T(1,128)S(1)}, f32[6,1,2048]{2,1,0:T(1,128)S(1)}, u32[]{:S(2)}, u32[]{:S(2)}) collective-permute-start(f32[6,1,2048]{2,1,0:T(1,128)S(1)} %get-tuple-element.140), channel_id=1, source_target_pairs={{0,4},{4,8},{8,12},{12,16},{16,20},{20,24},{24,28},{28,0},{1,5},{5... | collective-permute-start | bytes 147464 | tf_op jit(solution)/shard_map/ppermute | solution.py:20
  138.2 5.1 %collective-permute-start.21 = (f32[6,1,2048]{2,1,0:T(1,128)S(1)}, f32[6,1,2048]{2,1,0:T(1,128)S(1)}, u32[]{:S(2)}, u32[]{:S(2)}) collective-permute-start(f32[6,1,2048]{2,1,0:T(1,128)S(1)} %get-tuple-element.141), channel_id=1, source_target_pairs={{4,0},{8,4},{12,8},{16,12},{20,16},{24,20},{28,24},{0,28},{5,1},{9... | collective-permute-start | bytes 147464 | tf_op jit(solution)/shard_map/ppermute | solution.py:22
  144.5 1.8 collective-permute-start.23
  144.5 4.0 collective-permute-start.22
  152.8 63.4 %copy-start.23 = (f32[1,8,2048]{2,1,0:T(8,128)}, f32[1,8,2048]{2,1,0:T(8,128)S(1)}, u32[]{:S(2)}) copy-start(f32[1,8,2048]{2,1,0:T(8,128)S(1)} %get-tuple-element.174) | copy-start | bytes 196612
  198.9 6.6 %collective-permute-start.24 = (f32[3,1,2048]{2,1,0:T(1,128)S(1)}, f32[3,1,2048]{2,1,0:T(1,128)S(1)}, u32[]{:S(2)}, u32[]{:S(2)}) collective-permute-start(f32[3,1,2048]{2,1,0:T(1,128)S(1)} %get-tuple-element.156), channel_id=1, source_target_pairs={{0,4},{4,8},{8,12},{12,16},{16,20},{20,24},{24,28},{28,0},{1,5},{5... | collective-permute-start | bytes 73736 | tf_op jit(solution)/shard_map/ppermute | solution.py:20
  201.3 4.3 collective-permute-start.25
  206.4 1.5 collective-permute-start.27
  206.4 4.6 collective-permute-start.26
  216.3 6.9 %collective-permute-start.28 = (f32[6,1,2048]{2,1,0:T(1,128)S(1)}, f32[6,1,2048]{2,1,0:T(1,128)S(1)}, u32[]{:S(2)}, u32[]{:S(2)}) collective-permute-start(f32[6,1,2048]{2,1,0:T(1,128)S(1)} %get-tuple-element.136), channel_id=1, source_target_pairs={{0,4},{4,8},{8,12},{12,16},{16,20},{20,24},{24,28},{28,0},{1,5},{5... | collective-permute-start | bytes 147464 | tf_op jit(solution)/shard_map/ppermute | solution.py:20
  218.1 5.1 %collective-permute-start.29 = (f32[6,1,2048]{2,1,0:T(1,128)S(1)}, f32[6,1,2048]{2,1,0:T(1,128)S(1)}, u32[]{:S(2)}, u32[]{:S(2)}) collective-permute-start(f32[6,1,2048]{2,1,0:T(1,128)S(1)} %get-tuple-element.137), channel_id=1, source_target_pairs={{4,0},{8,4},{12,8},{16,12},{20,16},{24,20},{28,24},{0,28},{5,1},{9... | collective-permute-start | bytes 147464 | tf_op jit(solution)/shard_map/ppermute | solution.py:22
  224.4 1.8 collective-permute-start.31
  224.4 3.9 collective-permute-start.30
  279.0 6.6 %collective-permute-start.32 = (f32[3,1,2048]{2,1,0:T(1,128)S(1)}, f32[3,1,2048]{2,1,0:T(1,128)S(1)}, u32[]{:S(2)}, u32[]{:S(2)}) collective-permute-start(f32[3,1,2048]{2,1,0:T(1,128)S(1)} %get-tuple-element.154), channel_id=1, source_target_pairs={{0,4},{4,8},{8,12},{12,16},{16,20},{20,24},{24,28},{28,0},{1,5},{5... | collective-permute-start | bytes 73736 | tf_op jit(solution)/shard_map/ppermute | solution.py:20
  281.3 4.3 collective-permute-start.33
  286.4 1.5 collective-permute-start.35
  286.4 4.2 collective-permute-start.34
  295.9 6.9 %collective-permute-start.36 = (f32[6,1,2048]{2,1,0:T(1,128)S(1)}, f32[6,1,2048]{2,1,0:T(1,128)S(1)}, u32[]{:S(2)}, u32[]{:S(2)}) collective-permute-start(f32[6,1,2048]{2,1,0:T(1,128)S(1)} %get-tuple-element.132), channel_id=1, source_target_pairs={{0,4},{4,8},{8,12},{12,16},{16,20},{20,24},{24,28},{28,0},{1,5},{5... | collective-permute-start | bytes 147464 | tf_op jit(solution)/shard_map/ppermute | solution.py:20
  297.7 5.1 %collective-permute-start.37 = (f32[6,1,2048]{2,1,0:T(1,128)S(1)}, f32[6,1,2048]{2,1,0:T(1,128)S(1)}, u32[]{:S(2)}, u32[]{:S(2)}) collective-permute-start(f32[6,1,2048]{2,1,0:T(1,128)S(1)} %get-tuple-element.133), channel_id=1, source_target_pairs={{4,0},{8,4},{12,8},{16,12},{20,16},{24,20},{28,24},{0,28},{5,1},{9... | collective-permute-start | bytes 147464 | tf_op jit(solution)/shard_map/ppermute | solution.py:22
  303.1 1.8 collective-permute-start.39
  303.1 4.0 collective-permute-start.38
  352.7 6.6 %collective-permute-start.40 = (f32[3,1,2048]{2,1,0:T(1,128)S(1)}, f32[3,1,2048]{2,1,0:T(1,128)S(1)}, u32[]{:S(2)}, u32[]{:S(2)}) collective-permute-start(f32[3,1,2048]{2,1,0:T(1,128)S(1)} %get-tuple-element.152), channel_id=1, source_target_pairs={{0,4},{4,8},{8,12},{12,16},{16,20},{20,24},{24,28},{28,0},{1,5},{5... | collective-permute-start | bytes 73736 | tf_op jit(solution)/shard_map/ppermute | solution.py:20
  355.0 4.3 collective-permute-start.41
  359.4 1.5 collective-permute-start.43
  359.4 4.5 collective-permute-start.42
  380.1 105.7 %all-reduce.11.cloned.1.call-start = ((), (), s32[]{:S(2)}) async-start(), calls=%async_computation.1 | async-start | bytes 393216 | tf_op jit(solution)/shard_map/psum | solution.py:172
  (31 other events, 310.5 us)
Sparse Core Ops, SparseCore 0:
  380.2 72.0 all-reduce.8
  454.7 31.1 all-reduce.10
